TPU v7x, 256 devices: a whole 4x4x8 slice. The times are simulated.
256 devices in a mesh: wide: 32 (over x, z), narrow: 8 (over y, core).
Axes of the slice: x: 4, y: 4, z: 8, core: 2. Of those that a mesh axis runs over, the one named last changes fastest.
Arguments:
- hidden_in: bfloat16 [16384, 1664], P(('wide', 'narrow')), may hold values from -3 to 3
- queries: bfloat16 [16, 1024, 1664], P('narrow', 'wide'), may hold values from -24 to 24
- keys: bfloat16 [16, 1024, 1664], P('narrow', 'wide'), may hold values from -24 to 24
- values: bfloat16 [16, 1024, 1664], P('narrow', 'wide'), may hold values from -12 to 12
- out_weight: bfloat16 [1664, 1664], P('narrow', 'wide'), may hold values from -0.25 to 0.25
- merge_weight: bfloat16 [4, 1664, 1664], P(None, 'narrow', 'wide'), may hold values from -0.125 to 0.125
- segment_ids: int32 [4096], P('wide'), may hold values from 0 to 15, never falling along the last dimension, each value on 1 to 2560 neighbouring positions
- owners: int32 [4096, 1], P('wide'), may hold values from 0 to 31; in each aligned block of 128 rows (0 to 127, 128 to 255, ...) at most 8 rows name the same one
Outputs:
- hidden_out: bfloat16 [16384, 1664], P(('wide', 'narrow'))
- delivered: bfloat16 [8192, 1664], P('wide', 'narrow')
Inputs may be any that keep to these rules, and one draw needn't show every extreme that they name: `segment_ids`: never falling along the tokens; the largest image or clip holds exactly 2560 merged tokens. `owners`: among the merged tokens of one index of wide, at most 8 share an owner, and exactly 8 do for some owner.
All inputs are finite; a program needn't handle non-finite values.
Results may differ from a plain program's by a relative error of at most 0.025.
Values may be sent and summed in bfloat16 or wider, within the bound.
A program may use at most 64 MiB of HBM per device.

v0:
```python
import math

import jax
import jax.numpy as jnp
from jax import lax
from jax.sharding import PartitionSpec as P

HEAD_DIM = 104


NEG = -1e30


def shards(hidden_in, queries, keys, values, out_weight, merge_weight, segment_ids, owners):
    heads_here, packed_rows, packed_width = queries.shape
    tok_rows = packed_rows * 16
    local_width = heads_here * HEAD_DIM
    scale = 1.0 / math.sqrt(HEAD_DIM)
    tok_seg = jnp.repeat(segment_ids, 4)
    seg_packed = tok_seg.reshape(1, packed_rows, 16)
    gathered_out, gathered_merge = (
        lax.all_gather(out_weight, "wide", axis=1, tiled=True),
        lax.all_gather(merge_weight, "wide", axis=2, tiled=True),
    )
    query_heads = queries.reshape(heads_here, tok_rows, HEAD_DIM)

    def key_block(carry, key_rows, value_rows, seg_rows):
        keep = tok_seg[:, None] == seg_rows[None, :]
        best, total, accum = carry
        key_heads = key_rows.reshape(heads_here, -1, HEAD_DIM)
        value_heads = value_rows.reshape(heads_here, -1, HEAD_DIM)
        scores = (
            jnp.einsum("hqd,hkd->hqk", query_heads, key_heads, preferred_element_type=jnp.float32)
            * scale
        )
        scores = jnp.where(keep[None], scores, NEG)
        new_best = jnp.maximum(best, jnp.max(scores, axis=-1))
        weights = jnp.where(keep[None], jnp.exp(scores - new_best[..., None]), 0.0)
        factor = jnp.exp(best - new_best)
        total = total * factor + jnp.sum(weights, axis=-1)
        accum = accum * factor[..., None] + jnp.einsum(
            "hqk,hkd->hqd",
            weights.astype(jnp.bfloat16),
            value_heads,
            preferred_element_type=jnp.float32,
        )
        return (new_best, total, accum)

    start_state = (
        jnp.full((heads_here, tok_rows), NEG, jnp.float32),
        jnp.zeros((heads_here, tok_rows), jnp.float32),
        jnp.zeros((heads_here, tok_rows, HEAD_DIM), jnp.float32),
    )
    carry = start_state
    key_rows = lax.all_gather(keys, "wide", axis=1, tiled=True)
    value_rows = lax.all_gather(values, "wide", axis=1, tiled=True)
    seg_rows = lax.all_gather(seg_packed, "wide", axis=1, tiled=True)
    count = key_rows.shape[1]
    blocks = count // 32
    stacked = (
        key_rows.reshape(heads_here, blocks, 32, packed_width).transpose(1, 0, 2, 3),
        value_rows.reshape(heads_here, blocks, 32, packed_width).transpose(1, 0, 2, 3),
        seg_rows.reshape(blocks, 512),
    )

    def step_block(state, item):
        return (key_block(state, item[0], item[1], item[2]), None)

    carry, unused = lax.scan(step_block, carry, stacked)
    best, total, accum = carry
    attn = (
        (accum / total[..., None])
        .transpose(1, 0, 2)
        .reshape(tok_rows, local_width)
        .astype(jnp.bfloat16)
    )
    partial_mix = jnp.dot(attn, gathered_out, preferred_element_type=jnp.float32)
    summed_mix = lax.psum_scatter(
        partial_mix.astype(jnp.bfloat16), "narrow", scatter_dimension=0, tiled=True
    ).astype(jnp.float32)
    hidden_out = (hidden_in.astype(jnp.float32) + summed_mix).astype(jnp.bfloat16)
    whole_rows = lax.all_gather(hidden_out, "narrow", axis=0, tiled=True)
    my_columns = lax.dynamic_slice_in_dim(
        whole_rows, lax.axis_index("narrow") * local_width, local_width, 1
    )
    merged_rows = tok_rows // 4
    grouped = my_columns.reshape(merged_rows, 4, local_width)
    partial_feat = jnp.einsum(
        "gjc,jco->go", grouped, gathered_merge, preferred_element_type=jnp.float32
    )
    feature = lax.psum_scatter(
        partial_feat.astype(jnp.bfloat16), "narrow", scatter_dimension=1, tiled=True
    )
    owner_count = lax.axis_size("wide")
    capacity = 2 * merged_rows // owner_count
    owner_col = owners[:, 0]
    onehot = (owner_col[:, None] == jnp.arange(owner_count, dtype=jnp.int32)[None, :]).astype(
        jnp.int32
    )
    rank = jnp.sum(jnp.cumsum(onehot, axis=0) * onehot, axis=1) - 1
    slot = owner_col * capacity + rank
    picker = (jnp.arange(owner_count * capacity, dtype=jnp.int32)[:, None] == slot[None, :]).astype(
        jnp.bfloat16
    )
    outgoing = jnp.dot(picker, feature, preferred_element_type=jnp.float32).astype(jnp.bfloat16)
    outgoing = outgoing.reshape(owner_count, capacity, feature.shape[1])
    arrived = lax.all_to_all(outgoing, "wide", split_axis=0, concat_axis=0, tiled=True)
    return (hidden_out, arrived.reshape(owner_count * capacity, feature.shape[1]))


def solution(mesh):
    return jax.shard_map(
        shards,
        mesh=mesh,
        in_specs=(
            P(("wide", "narrow"), None),
            P("narrow", "wide", None),
            P("narrow", "wide", None),
            P("narrow", "wide", None),
            P("narrow", "wide"),
            P(None, "narrow", "wide"),
            P("wide"),
            P("wide", None),
        ),
        out_specs=(P(("wide", "narrow"), None), P("wide", "narrow")),
        check_vma=False,
    )
```

profile of v0, /device:TPU:1, one launch (start us, length us, event | category | flops | bytes accessed | tf_op | source)
XLA Modules:
  0.0 574.0 jit_solution(16896971549550113275)
XLA Ops:
  9.7 44.1 %all_gather.18 = s32[1,1024,16]{2,0,1:T(1,128)S(1)} all-gather(s32[1,32,16]{2,0,1:T(1,128)S(1)} %copy.25), channel_id=1, replica_groups=mesh['wide'=32,'narrow'=8] {'wide'}, dimensions={1}, use_global_device_ids=true | all-gather | bytes 67584 | tf_op jit(solution)/shard_map/all_gather | solution.py:57
  54.3 2.0 reduce.3
  57.2 41.2 %all-gather = bf16[32,52,208]{2,1,0:T(8,128)(2,1)S(1)} all-gather(bf16[1,52,208]{2,1,0:T(8,128)(2,1)S(1)} %bitcast.77), channel_id=1, replica_groups=mesh['wide'=32,'narrow'=8] {'wide'}, dimensions={0}, use_global_device_ids=true | all-gather | bytes 713856 | tf_op jit(solution)/shard_map/all_gather | solution.py:22
  98.5 1.3 reshape.93
  99.7 9.4 %all-gather.6.cloned.1.call-done = bf16[2,1024,1664]{2,1,0:T(8,128)(2,1)} async-done(((bf16[2,32,1664]{2,1,0:T(8,128)(2,1)}), bf16[2,1024,1664]{2,1,0:T(8,128)(2,1)}) %all-gather.6.cloned.1.call-update) | async-done | bytes 6815760 | tf_op jit(solution)/shard_map/all_gather | solution.py:55
  109.2 90.5 %all-gather.8.cloned.1.call-done = bf16[2,1024,1664]{2,1,0:T(8,128)(2,1)} async-done(((bf16[2,32,1664]{2,1,0:T(8,128)(2,1)}), bf16[2,1024,1664]{2,1,0:T(8,128)(2,1)}) %all-gather.8.cloned.1.call-update) | async-done | bytes 6815760 | tf_op jit(solution)/shard_map/all_gather | solution.py:56
  199.7 167.4 %while.15 = (s32[]{:T(128)}, f32[2,512]{1,0:T(2,128)S(1)}, f32[2,512]{1,0:T(2,128)S(1)}, f32[2,512,104]{1,2,0:T(8,128)S(1)}, s32[32,512]{1,0:T(8,128)S(1)}, /*in...) while((s32[]{:T(128)}, f32[2,512]{1,0:T(2,128)S(1)}, ...), condition=%wide.region_3.4_spmd.clone, body=%wide.region_0.3_spmd.clone.sunk | while | flops 225506304 | bytes 10615425 | solution.py:69
  200.8 1.1 dynamic-slice_bitcast_fusion.3
  206.0 1.1 dynamic-slice_bitcast_fusion.3
  211.3 1.1 dynamic-slice_bitcast_fusion.3
  216.5 1.1 dynamic-slice_bitcast_fusion.3
  221.7 1.1 dynamic-slice_bitcast_fusion.3
  227.0 1.1 dynamic-slice_bitcast_fusion.3
  232.2 1.1 dynamic-slice_bitcast_fusion.3
  237.4 1.1 dynamic-slice_bitcast_fusion.3
  242.7 1.1 dynamic-slice_bitcast_fusion.3
  247.9 1.1 dynamic-slice_bitcast_fusion.3
  253.1 1.1 dynamic-slice_bitcast_fusion.3
  258.4 1.1 dynamic-slice_bitcast_fusion.3
  263.6 1.1 dynamic-slice_bitcast_fusion.3
  268.8 1.1 dynamic-slice_bitcast_fusion.3
  274.1 1.1 dynamic-slice_bitcast_fusion.3
  279.3 1.1 dynamic-slice_bitcast_fusion.3
  284.5 1.1 dynamic-slice_bitcast_fusion.3
  289.8 1.1 dynamic-slice_bitcast_fusion.3
  295.0 1.1 dynamic-slice_bitcast_fusion.3
  300.2 1.1 dynamic-slice_bitcast_fusion.3
  305.4 1.1 dynamic-slice_bitcast_fusion.3
  310.7 1.1 dynamic-slice_bitcast_fusion.3
  315.9 1.1 dynamic-slice_bitcast_fusion.3
  321.1 1.1 dynamic-slice_bitcast_fusion.3
  326.4 1.1 dynamic-slice_bitcast_fusion.3
  331.6 1.1 dynamic-slice_bitcast_fusion.3
  336.8 1.1 dynamic-slice_bitcast_fusion.3
  342.1 1.1 dynamic-slice_bitcast_fusion.3
  347.3 1.1 dynamic-slice_bitcast_fusion.3
  352.5 1.1 dynamic-slice_bitcast_fusion.3
  357.8 1.1 dynamic-slice_bitcast_fusion.3
  363.0 1.1 dynamic-slice_bitcast_fusion.3
  367.2 3.1 convolution_convert_fusion
  370.4 30.7 %reduce-scatter.5.cloned.1.call-done = bf16[64,1664]{1,0:T(8,128)(2,1)} async-done(((bf16[512,1664]{1,0:T(8,128)(2,1)}), bf16[64,1664]{1,0:T(8,128)(2,1)}) %reduce-scatter.5.cloned.1.call-update) | async-done | bytes 213008 | tf_op jit(solution)/shard_map/reduce_scatter | solution.py:78
  401.1 1.7 add_convert_fusion
  403.4 29.2 %all-gather.10.cloned.1.call-done = bf16[512,1664]{1,0:T(8,128)(2,1)} async-done(((bf16[64,1664]{1,0:T(8,128)(2,1)}), bf16[512,1664]{1,0:T(8,128)(2,1)}) %all-gather.10.cloned.1.call-update) | async-done | bytes 1703952 | tf_op jit(solution)/shard_map/all_gather | solution.py:82
  432.6 1.1 constant_dynamic-slice_fusion.1
  433.8 78.2 %all-gather.12.cloned.1.call-done = bf16[4,208,1664]{1,0,2:T(4,128)(2,1)} async-done(((bf16[4,208,52]{1,0,2:T(4,128)(2,1)}), bf16[4,208,1664]{1,0,2:T(4,128)(2,1)}) %all-gather.12.cloned.1.call-update) | async-done | bytes 2768912 | tf_op jit(solution)/shard_map/all_gather | solution.py:23
  512.0 3.8 fusion.23
  516.2 30.8 %reduce-scatter.7.cloned.1.call-done = bf16[208,128]{1,0:T(8,128)(2,1)} async-done(((bf16[1664,128]{1,0:T(8,128)(2,1)}), bf16[208,128]{1,0:T(8,128)(2,1)}) %reduce-scatter.7.cloned.1.call-update) | async-done | bytes 53264
  548.1 18.3 %all_to_all.5 = bf16[32,8,208]{2,1,0:T(8,128)(2,1)S(1)} all-to-all(bf16[32,8,208]{2,1,0:T(8,128)(2,1)S(1)} %bitcast.71), channel_id=1, replica_groups=mesh['wide'=32,'narrow'=8] {'wide'}, dimensions={0} | all-to-all | bytes 212992 | tf_op jit(solution)/shard_map/all_to_all | solution.py:107
  (424 shorter events, 137.0 us)
Async XLA Ops:
  7.2 49.4 %copy-start.1 = (bf16[2,32,1664]{2,1,0:T(8,128)(2,1)S(1)}, bf16[2,32,1664]{2,1,0:T(8,128)(2,1)}, u32[]{:S(2)}) copy-start(bf16[2,32,1664]{2,1,0:T(8,128)(2,1)} %param.11) | copy-start | bytes 638980
  7.2 50.0 %copy-start.2 = (bf16[208,52]{0,1:T(8,128)(2,1)S(1)}, bf16[208,52]{0,1:T(8,128)(2,1)}, u32[]{:S(2)}) copy-start(bf16[208,52]{0,1:T(8,128)(2,1)} %param.14) | copy-start | bytes 64900
  7.2 102.0 %all-gather.6.cloned.1.call-start = ((), (), s32[]{:S(2)}) async-start(), calls=%async_computation.3 | async-start | bytes 7028736 | tf_op jit(solution)/shard_map/all_gather | solution.py:55
  7.9 191.8 %all-gather.8.cloned.1.call-start = ((), (), s32[]{:S(2)}) async-start(), calls=%async_computation.4 | async-start | bytes 7028736 | tf_op jit(solution)/shard_map/all_gather | solution.py:56
  8.7 392.4 %reduce-scatter.5.cloned.1.call-start = ((), (), s32[]{:S(2)}) async-start(), calls=%async_computation.5 | async-start | bytes 1916928 | tf_op jit(solution)/shard_map/reduce_scatter | solution.py:78
  367.2 33.9 %copy-start = (bf16[64,1664]{1,0:T(8,128)(2,1)S(1)}, bf16[64,1664]{1,0:T(8,128)(2,1)}, u32[]{:S(2)}) copy-start(bf16[64,1664]{1,0:T(8,128)(2,1)} %param.10) | copy-start | bytes 638980
  370.3 62.2 %all-gather.10.cloned.1.call-start = ((), (), s32[]{:S(2)}) async-start(), calls=%async_computation.6 | async-start | bytes 1916928 | tf_op jit(solution)/shard_map/all_gather | solution.py:82
  402.7 109.2 %all-gather.12.cloned.1.call-start = ((), (), s32[]{:S(2)}) async-start(), calls=%async_computation.7 | async-start | bytes 3514368 | tf_op jit(solution)/shard_map/all_gather | solution.py:23
  403.3 143.7 %reduce-scatter.7.cloned.1.call-start = ((), (), s32[]{:S(2)}) async-start(), calls=%async_computation.8 | async-start | bytes 479232
  433.8 82.0 %copy-start.3 = (s32[128,1]{0,1:T(1,128)S(1)}, s32[128,1]{0,1:T(1,128)}, u32[]{:S(2)}) copy-start(s32[128,1]{0,1:T(1,128)} %param.17) | copy-start | bytes 1540
Sparse Core Ops, SparseCore 0:
  10.6 98.5 all-gather.5
  111.8 87.9 all-gather.7
  370.4 30.5 reduce-scatter.4
  403.5 29.0 all-gather.9
  435.3 76.6 all-gather.11
  515.9 31.0 reduce-scatter.6
where the time goes:
time: 578 us; the launch traced here: 574 us
  waiting for transfers between devices  271 us (47%)
  blocking collectives  104 us (18%)
  local copies, waits for them, and re-layouts  101 us (17%)
  matrix products  50.8 us (9%)
  other arithmetic  30.1 us (5%)
  between operations  14.3 us (2%)
    all_gather x1, waiting for transfers between devices, shards(): value_rows = lax.all_gather(values, 'wide', axis=1, tiled=True)  90.5 us
    all_gather x1, waiting for transfers between devices, shards(): lax.all_gather(merge_weight, 'wide', axis=2, tiled=True)  78.2 us
    all_gather x1, blocking collectives, shards(): seg_rows = lax.all_gather(seg_packed, 'wide', axis=1, tiled=True)  44.1 us
    all_gather x1, blocking collectives, shards(): lax.all_gather(out_weight, 'wide', axis=1, tiled=True)  41.2 us
    dynamic_slice x64, local copies, waits for them, and re-layouts, shards(): carry, unused = lax.scan(step_block, carry, stacked)  34.9 us
    unnamed x7, waiting for transfers between devices  32.7 us
    reduce_scatter x1, waiting for transfers between devices, shards(): lax.psum_scatter(partial_mix.astype(jnp.bfloat16), 'narrow', scatter_dime...  30.7 us
    all_gather x1, waiting for transfers between devices, shards(): whole_rows = lax.all_gather(hidden_out, 'narrow', axis=0, tiled=True)  29.2 us
  transfers between devices with their start and end apart: 6, of which 6 were waited for; matrix products, arithmetic and copies ran while one was open for 1% of the time, Pallas kernels for 0%

commit v1 on v0

v1 whole, which is shorter than its diff:
```python
import math

import jax
import jax.numpy as jnp
from jax import lax
from jax.experimental import pallas as pl
from jax.experimental.pallas import tpu as pltpu
from jax.sharding import PartitionSpec as P

HD = 104
X, Z, Y = 4, 8, 4
NW, NN = 32, 8
D = 1664
TILE = 2048
BIG = 2.0**100
bf16, f32, i32 = jnp.bfloat16, jnp.float32, jnp.int32
MESH = pl.DeviceIdType.MESH


def iota(shape, dim):
    return lax.broadcasted_iota(i32, shape, dim)


def kernel(q_ref, k_ref, v_ref, seg_ref, own_ref, hin_ref, wout_ref, wm_ref,
           hout_ref, dout_ref,
           kv, qb, oh, tr, kx, vx, qx, m_s, acc_s, ob, orecv, hb, hrecv, fb, frecv, outg, drecv,
           s0, r_kv, r_q, r_oh, ss, rs, dss, drs, so, ro, sh, rh, sf, rf, sd, rd):
    w = lax.axis_index("wide")
    n = lax.axis_index("narrow")
    x, z = w // Z, w % Z
    y, c = n // 2, n % 2
    up = 1 - 2 * c
    scale = math.log2(math.e) / math.sqrt(HD)

    def is_me(dw, dn):
        return (dw == w) & (dn == n)

    def remote(src, dst, ssem, rsem, dw, dn):
        return pltpu.make_async_remote_copy(src_ref=src, dst_ref=dst, send_sem=ssem, recv_sem=rsem,
                                            device_id=(dw, dn), device_id_type=MESH)

    def send(src, dst, ssem, rsem, dw, dn):
        @pl.when(jnp.logical_not(is_me(dw, dn)))
        def _():
            remote(src, dst, ssem, rsem, dw, dn).start()

        @pl.when(is_me(dw, dn))
        def _():
            pltpu.make_async_copy(src, dst, rsem).start()

    def sent(src, ssem, dw, dn):
        @pl.when(jnp.logical_not(is_me(dw, dn)))
        def _():
            remote(src, src, ssem, ssem, dw, dn).wait_send()

    def arrived(dst, rsem):
        remote(dst, dst, rsem, rsem, w, n).wait_recv()

    barrier = pltpu.get_barrier_semaphore()

    @pl.loop(0, X * NN)
    def _(i):
        dw, dn = (i // NN) * Z + z, i % NN

        @pl.when(jnp.logical_not(is_me(dw, dn)))
        def _():
            pl.semaphore_signal(barrier, inc=1, device_id=(dw, dn), device_id_type=MESH)

    @pl.loop(0, NW)
    def _(i):
        @pl.when(i % Z != z)
        def _():
            pl.semaphore_signal(barrier, inc=1, device_id=(i, n), device_id_type=MESH)

    t = (iota((128, 128), 0) == seg_ref[...] + 32 * (iota((1, 128), 1) & 3)).astype(f32)
    tr[...] = t.T
    oh[...] = (tr[pl.ds(0, 32, stride=4), :] + tr[pl.ds(1, 32, stride=4), :]
               + tr[pl.ds(2, 32, stride=4), :] + tr[pl.ds(3, 32, stride=4), :]).astype(bf16)

    g64, p64 = iota((64, 64), 0), iota((64, 64), 1)
    perm = (p64 == 4 * (g64 & 15) + (g64 >> 4)).astype(bf16)
    hp = jnp.dot(perm, hin_ref[...], preferred_element_type=f32).astype(bf16)
    hb[...] = jnp.zeros_like(hb)
    for i in range(NN):
        hb[i, :, 0:208] = hp[:, 208 * i:208 * i + 208]

    owner_row = own_ref[...]
    owner_col = jnp.broadcast_to(owner_row.astype(f32), (128, 128)).T
    same = (owner_col == owner_row.astype(f32)) & (iota((128, 128), 0) < iota((128, 128), 1))
    rank = jnp.sum(same.astype(f32), axis=0, keepdims=True)
    slot_of = owner_row * 8 + rank.astype(i32)
    picker = (iota((256, 128), 0) == slot_of).astype(bf16)

    pl.semaphore_wait(barrier, X * NN - 1 + NW - X)

    rows_x = pl.ds(pl.multiple_of(32 * x, 32), 32)
    rows_q = pl.ds(pl.multiple_of(16 * x, 16), 16)
    main, tail = pl.ds(0, D), pl.ds(D, 128)
    starts = []
    for i in range(2):
        dw = (2 * c + i) * Z + z
        starts.append((k_ref.at[i], kv.at[0, z, rows_x, main], s0.at[i], r_kv.at[x], dw, 2 * y))
        starts.append((v_ref.at[i], kv.at[1, z, rows_x, main], s0.at[2 + i], r_kv.at[x], dw, 2 * y + 1))
    for i in range(2):
        dw = (2 * c + i) * Z + z
        for d in range(2):
            starts.append((q_ref.at[i, pl.ds(16 * d, 16)], qb.at[rows_q], s0.at[4 + 2 * i + d], r_q.at[x], dw,
                           2 * y + d))
    for dx in range(X):
        starts.append((oh, kv.at[c, z, rows_x, tail], s0.at[8 + dx], r_oh.at[x], dx * Z + z, n))
    for args in starts:
        send(*args)

    m_s[...] = jnp.full_like(m_s, -3e38)
    acc_s[...] = jnp.zeros_like(acc_s)

    lane = iota((128, 128), 1)
    ones_col = (lane == HD).astype(bf16)

    def piece(ref_slice, j):
        t, r = (HD * j) // 128, (HD * j) % 128
        out = ref_slice(t)
        if r:
            out = pltpu.roll(out, 128 - r, 1)
        if r + HD > 128:
            nxt = pltpu.roll(ref_slice(t + 1), 128 - r, 1)
            out = jnp.where(iota(out.shape, 1) < 128 - r, out, nxt)
        return out

    def attend(slot):
        ohs = kv[0, slot, :, D:D + 128]
        for jj in range(4):
            ohr = pltpu.roll(ohs, (HD - 32 * jj) % 128, 1)
            for j in range(4 * jj, 4 * jj + 4):
                kj = piece(lambda t: kv[0, slot, :, 128 * t:128 * t + 128], j)
                kx[128 * j:128 * j + 128, :] = jnp.where(lane < HD, kj, ohr)
                vj = piece(lambda t: kv[1, slot, :, 128 * t:128 * t + 128], j)
                vx[128 * j:128 * j + 128, :] = jnp.where(lane < HD, vj, ones_col)

        @pl.loop(0, X)
        def _(qt):
            rows = pl.ds(pl.multiple_of(256 * qt, 256), 256)
            s = lax.dot_general(qx[rows, :], kx[...], (((1,), (1,)), ((), ())), preferred_element_type=f32)
            m_old = m_s[rows, :]
            m_new = jnp.maximum(m_old, jnp.max(s, axis=1, keepdims=True))
            p = jnp.exp2((s - m_new) * scale).astype(bf16)
            fix = jnp.exp2((m_old - m_new) * scale)
            acc_s[rows, :] = acc_s[rows, :] * fix + jnp.dot(p, vx[...], preferred_element_type=f32)
            m_s[rows, :] = m_new

    for i in range(X):
        arrived(kv.at[c, z, pl.ds(32 * i, 32), main], r_kv.at[i])
        arrived(kv.at[c, z, pl.ds(32 * i, 32), tail], r_oh.at[i])

    def slot_at(k):
        h = (k + 1) // 2
        sign = jnp.where(k % 2 == 1, -1, 1)
        return (z + sign * up * h + 2 * Z) % Z

    def to_partner(slot):
        return remote(kv.at[c, slot], kv.at[c, slot], dss.at[slot], drs.at[slot], w, n + up)

    def onward(k, t):
        slot = slot_at(k)
        step = jnp.where(t % 2 == 1, up, -up)
        dz = (z + step + Z) % Z
        return remote(kv.at[c, slot], kv.at[c, slot], ss.at[t], rs.at[t], x * Z + dz, n)

    onward(0, 1).start()
    onward(0, 2).start()
    to_partner(z).start()

    for i in range(X):
        arrived(qb.at[pl.ds(16 * i, 16)], r_q.at[i])
    lane16 = iota((16, 128), 1)
    for i in range(X):
        ohq = kv[c, z, pl.ds(pl.multiple_of(32 * i + 16 * c, 16), 16), D:D + 128]
        for jj in range(4):
            ohr = (pltpu.roll(ohq, (HD - 32 * jj) % 128, 1) - bf16(1)) * bf16(BIG)
            ohr = jnp.where(lane16 < HD + 16, ohr, bf16(0))
            for j in range(4 * jj, 4 * jj + 4):
                qj = piece(lambda t: qb[16 * i:16 * i + 16, 128 * t:128 * t + 128], j)
                qx[256 * i + 16 * j:256 * i + 16 * j + 16, :] = jnp.where(lane16 < HD, qj, ohr)

    @pl.loop(0, Z)
    def _(k):
        def take(kk):
            slot = slot_at(kk)
            arrived(kv.at[c, slot], rs.at[kk])

            @pl.when(kk + 2 < Z)
            def _():
                onward(kk, kk + 2).start()
            to_partner(slot).start()

        @pl.when(k % 2 == 1)
        def _():
            take(k)

            @pl.when(k + 1 < Z)
            def _():
                take(k + 1)
        slot = slot_at(k)
        arrived(kv.at[1 - c, slot], drs.at[slot])
        attend(slot)

    i0, i1 = iota((256, 256), 0), iota((256, 256), 1)
    grp, pos = i0 & 15, (i0 >> 4) & 3
    r_src = 4 * (i0 >> 6) + (grp >> 2)
    j_src = 4 * (grp & 3) + pos
    perm256 = (i1 == j_src * 16 + r_src).astype(bf16)
    lane256 = iota((256, 128), 1)
    for i in range(X):
        a = acc_s[256 * i:256 * i + 256, :]
        a = jnp.where(lane256 < HD, a / a[:, HD:HD + 1], 0.0).astype(bf16)
        ob[4 * i:4 * i + 4] = jnp.dot(perm256, a, preferred_element_type=f32).astype(bf16).reshape(4, 64, 128)
    head = 4 * y + x
    for i in range(X):
        for l in range(4):
            send(ob.at[4 * i + l], orecv.at[head], so.at[4 * i + l], ro.at[head], i * Z + z, 4 * c + l)

    hid = jnp.zeros((64, TILE), f32)
    for hp2 in range(8):
        arrived(orecv.at[2 * hp2], ro.at[2 * hp2])
        arrived(orecv.at[2 * hp2 + 1], ro.at[2 * hp2 + 1])
        a = jnp.concatenate([orecv[2 * hp2], orecv[2 * hp2 + 1]], axis=1)
        hid = hid + jnp.dot(a, wout_ref[256 * hp2:256 * hp2 + 256, :], preferred_element_type=f32)
    for i in range(NN):
        hb[i] = (hb[i].astype(f32) + hid[:, 256 * i:256 * i + 256]).astype(bf16)
    for i in range(NN):
        send(hb.at[i], hrecv.at[n], sh.at[i], rh.at[n], w, i)
    whole = jnp.concatenate([hb[i][:, 0:208] for i in range(NN)], axis=1)
    back = (g64 == 4 * (p64 & 15) + (p64 >> 4)).astype(bf16)
    hout_ref[...] = jnp.dot(back, whole, preferred_element_type=f32).astype(bf16)

    for i in range(NN):
        arrived(hrecv.at[i], rh.at[i])
    part = jnp.zeros((128, TILE), f32)
    for j in range(4):
        part = part + jnp.dot(hrecv[:, 16 * j:16 * j + 16, :].reshape(128, 256), wm_ref[j],
                              preferred_element_type=f32)
    for i in range(NN):
        fb[i] = part[:, 256 * i:256 * i + 256].astype(bf16)
    for i in range(NN):
        send(fb.at[i], frecv.at[n], sf.at[i], rf.at[n], w, i)
    feat = jnp.zeros((128, 256), f32)
    for i in range(NN):
        arrived(frecv.at[i], rf.at[i])
        feat = feat + frecv[i].astype(f32)

    outg[...] = jnp.dot(picker, feat.astype(bf16), preferred_element_type=f32).reshape(NW, 8, 256).astype(bf16)

    @pl.loop(0, NW)
    def _(i):
        send(outg.at[i], drecv.at[w], sd.at[i], rd.at[w], i, n)

    @pl.loop(0, NW)
    def _(i):
        arrived(drecv.at[i], rd.at[i])
    dout_ref[...] = drecv[...].astype(f32).reshape(256, 256).astype(bf16)[:, 0:208]

    for src, dst, ssem, rsem, dw, dn in starts:
        sent(src, ssem, dw, dn)

    @pl.loop(1, Z)
    def _(t):
        onward(jnp.maximum(t - 2, 0), t).wait_send()

    @pl.loop(0, Z)
    def _(t):
        to_partner(t).wait_send()
    for i in range(X):
        for l in range(4):
            sent(ob.at[4 * i + l], so.at[4 * i + l], i * Z + z, 4 * c + l)
    for i in range(NN):
        sent(hb.at[i], sh.at[i], w, i)
        sent(fb.at[i], sf.at[i], w, i)

    @pl.loop(0, NW)
    def _(i):
        sent(outg.at[i], sd.at[i], i, n)


def shards(hidden_in, queries, keys, values, out_weight, merge_weight, segment_ids, owners):
    wout = lax.all_gather(out_weight, "wide", axis=1, tiled=True)
    wout = lax.all_gather(wout, "narrow", axis=0, tiled=True)
    wout = jnp.pad(wout.reshape(16, HD, NN, 208), ((0, 0), (0, 24), (0, 0), (0, 48))).reshape(TILE, TILE)
    wm = lax.all_gather(merge_weight, "wide", axis=2, tiled=True)
    wm = jnp.pad(wm.reshape(4, 208, NN, 208), ((0, 0), (0, 48), (0, 0), (0, 48))).reshape(4, 256, TILE)
    vm = pl.BlockSpec(memory_space=pltpu.VMEM)
    dma = pltpu.SemaphoreType.DMA
    return pl.pallas_call(
        kernel,
        out_shape=(jax.ShapeDtypeStruct((64, D), bf16), jax.ShapeDtypeStruct((256, 208), bf16)),
        in_specs=[vm] * 8,
        out_specs=(vm, vm),
        scratch_shapes=[
            pltpu.VMEM((2, Z, 128, D + 128), bf16),
            pltpu.VMEM((64, D), bf16),
            pltpu.VMEM((32, 128), bf16),
            pltpu.VMEM((128, 128), f32),
            pltpu.VMEM((2048, 128), bf16),
            pltpu.VMEM((2048, 128), bf16),
            pltpu.VMEM((1024, 128), bf16),
            pltpu.VMEM((1024, 1), f32),
            pltpu.VMEM((1024, 128), f32),
            pltpu.VMEM((16, 64, 128), bf16),
            pltpu.VMEM((16, 64, 128), bf16),
            pltpu.VMEM((NN, 64, 256), bf16),
            pltpu.VMEM((NN, 64, 256), bf16),
            pltpu.VMEM((NN, 128, 256), bf16),
            pltpu.VMEM((NN, 128, 256), bf16),
            pltpu.VMEM((NW, 8, 256), bf16),
            pltpu.VMEM((NW, 8, 256), bf16),
            dma((12,)), dma((X,)), dma((X,)), dma((X,)),
            dma((Z,)), dma((Z,)), dma((Z,)), dma((Z,)),
            dma((16,)), dma((16,)), dma((NN,)), dma((NN,)), dma((NN,)), dma((NN,)),
            dma((NW,)), dma((NW,)),
        ],
        compiler_params=pltpu.CompilerParams(collective_id=0, has_side_effects=True,
                                             vmem_limit_bytes=60 * 1024 * 1024),
    )(queries, keys, values, segment_ids.reshape(1, 128), owners.reshape(1, 128), hidden_in, wout, wm)


def solution(mesh):
    return jax.shard_map(
        shards,
        mesh=mesh,
        in_specs=(
            P(("wide", "narrow"), None),
            P("narrow", "wide", None),
            P("narrow", "wide", None),
            P("narrow", "wide", None),
            P("narrow", "wide"),
            P(None, "narrow", "wide"),
            P("wide"),
            P("wide", None),
        ),
        out_specs=(P(("wide", "narrow"), None), P("wide", "narrow")),
        check_vma=False,
    )
```

time: 578 us -> 283 us (0.49)
  waiting for transfers between devices: 271 us -> 65.8 us
  Pallas kernels: 0 us -> 106 us
  blocking collectives: 104 us -> 44.2 us
  matrix products: 50.8 us -> 0 us
  local copies, waits for them, and re-layouts: 101 us -> 52.6 us
  other arithmetic: 30.1 us -> 0 us
    all_gather x4 -> x2, waiting for transfers between devices: 207 us -> 65.1 us  [the longest x1 37.7 us: shards(): wm = lax.all_gather(merge_weight, 'wide', axis=2, tiled=True)]
    pallas_call x0 -> x1, Pallas kernels: none -> 106 us  [shards(): pl.pallas_call(kernel, out_shape=(jax.ShapeDtypeStruct((64, D), bf16), ja...]
    dot_general x67 -> x0, matrix products: 50.8 us -> none  [the longest x32 25.9 us: key_block(): jnp.einsum('hqk,hkd->hqd', weights.astype(jnp.bfloat16), value_heads, pre...]
    all_gather x2 -> x1, blocking collectives: 85.3 us -> 44.2 us  [shards(): wout = lax.all_gather(out_weight, 'wide', axis=1, tiled=True)]
    dynamic_slice x65 -> x0, local copies, waits for them, and re-layouts: 36 us -> none  [the longest x64 34.9 us: shards(): carry, unused = lax.scan(step_block, carry, stacked)]
    unnamed x7 -> x2, waiting for transfers between devices: 32.7 us -> 0.7 us
    reduce_scatter x1 -> x0, waiting for transfers between devices: 30.7 us -> none  [shards(): lax.psum_scatter(partial_mix.astype(jnp.bfloat16), 'narrow', scatter_dime...]
    broadcast_in_dim x36 -> x0, local copies, waits for them, and re-layouts: 24.3 us -> none  [shards(): tok_seg = jnp.repeat(segment_ids, 4)]
  transfers between devices with their start and end apart: 6 -> 2, of which waited for: 6 -> 2; matrix products, arithmetic and copies ran while one was open for 1% -> 6% of each run, Pallas kernels for 0% -> 0%
where the time goes in v1:
time: 283 us
  Pallas kernels  106 us (37%)
  waiting for transfers between devices  65.8 us (23%)
  local copies, waits for them, and re-layouts  52.6 us (19%)
  blocking collectives  44.2 us (16%)
  between operations  14.1 us (5%)
    pallas_call x1, Pallas kernels, shards(): pl.pallas_call(kernel, out_shape=(jax.ShapeDtypeStruct((64, D), bf16), ja...  106 us
    all_gather x1, blocking collectives, shards(): wout = lax.all_gather(out_weight, 'wide', axis=1, tiled=True)  44.2 us
    all_gather x1, waiting for transfers between devices, shards(): wm = lax.all_gather(merge_weight, 'wide', axis=2, tiled=True)  37.7 us
    all_gather x1, waiting for transfers between devices, shards(): wout = lax.all_gather(wout, 'narrow', axis=0, tiled=True)  27.4 us
    reshape x1, local copies, waits for them, and re-layouts, shards(): wout.reshape(16, HD, NN, 208)  14.7 us
    unnamed x4, local copies, waits for them, and re-layouts  13.4 us
    pad x1, local copies, waits for them, and re-layouts, shards(): jnp.pad(wout.reshape(16, HD, NN, 208), ((0, 0), (0, 24), (0, 0), (0, 48)))  7.56 us
    reshape x1, local copies, waits for them, and re-layouts, shards(): jnp.pad(wm.reshape(4, 208, NN, 208), ((0, 0), (0, 48), (0, 0), (0, 48)))  7.44 us
  transfers between devices with their start and end apart: 2, of which 2 were waited for; matrix products, arithmetic and copies ran while one was open for 6% of the time, Pallas kernels for 0%

profile of v1, /device:TPU:1, one launch (start us, length us, event | category | flops | bytes accessed | tf_op | source)
XLA Modules:
  0.0 282.6 jit_solution(2264233985439677030)
XLA Ops:
  7.2 0.0 all-gather.6.cloned.1.call-start
  7.2 0.7 all-gather.6.cloned.1.call-update
  7.9 0.0 all-gather.4.cloned.1.call-start
  7.9 44.2 %all-gather = bf16[32,52,208]{2,1,0:T(8,128)(2,1)S(1)} all-gather(bf16[1,52,208]{2,1,0:T(8,128)(2,1)} %bitcast.16), channel_id=1, replica_groups=mesh['wide'=32,'narrow'=8] {'wide'}, dimensions={0}, use_global_device_ids=true | all-gather | bytes 713856 | tf_op jit(solution)/shard_map/all_gather | solution.py:285
  52.1 0.4 reshape.29
  52.5 1.2 copy.16
  53.7 0.0 all-gather.4.cloned.1.call-update
  53.7 37.7 %all-gather.6.cloned.1.call-done = bf16[4,208,1664]{1,0,2:T(4,128)(2,1)} async-done(((bf16[4,208,52]{1,0,2:T(4,128)(2,1)}), bf16[4,208,1664]{1,0,2:T(4,128)(2,1)}) %all-gather.6.cloned.1.call-update) | async-done | bytes 2768912 | tf_op jit(solution)/shard_map/all_gather | solution.py:288
  91.4 5.2 %copy.17 = bf16[4,208,8,208]{3,2,1,0:T(8,128)(2,1)S(1)} copy(bf16[4,208,8,208]{1,0,3,2:T(4,128)(2,1)} %bitcast.15) | data formatting | bytes 5537792 | tf_op jit(solution)/shard_map/reshape | solution.py:289
  96.6 2.6 pad.9
  99.2 7.4 %reshape.27.wm_ref = bf16[4,256,2048]{2,1,0:T(8,128)(2,1)} reshape(bf16[4,256,8,256]{3,2,1,0:T(8,128)(2,1)} %pad.9) | data formatting | bytes 8388608 | tf_op jit(solution)/shard_map/reshape | solution.py:289
  106.6 27.4 %all-gather.4.cloned.1.call-done = bf16[1664,1664]{1,0:T(8,128)(2,1)} async-done(((bf16[208,1664]{1,0:T(8,128)(2,1)}), bf16[1664,1664]{1,0:T(8,128)(2,1)}) %all-gather.4.cloned.1.call-update) | async-done | bytes 5537808 | tf_op jit(solution)/shard_map/all_gather | solution.py:286
  134.1 14.7 %reshape.24 = bf16[16,104,8,208]{3,2,1,0:T(8,128)(2,1)} reshape(bf16[1664,1664]{1,0:T(8,128)(2,1)} %all-gather.4.cloned.1.call-done) | data formatting | bytes 11075584 | tf_op jit(solution)/shard_map/reshape | solution.py:287
  148.8 7.6 %pad.8 = bf16[16,128,8,256]{3,2,1,0:T(8,128)(2,1)} pad(bf16[16,104,8,208]{3,2,1,0:T(8,128)(2,1)} %reshape.24, bf16[]{:T(256)} %constant.2.clone.1), padding=0_0x0_24x0_0x0_48 | pad | bytes 13926402 | tf_op jit(solution)/shard_map/jit(_pad)/pad | solution.py:287
  156.3 10.3 %copy.19 = bf16[256,8,8,256]{3,1,2,0:T(8,128)(2,1)} copy(bf16[256,8,8,256]{3,2,1,0:T(8,128)(2,1)} %bitcast.13) | data formatting | bytes 16777216
  166.6 105.9 %shard_map.95 = (bf16[64,1664]{1,0:T(8,128)(2,1)}, bf16[256,208]{1,0:T(8,128)(2,1)}) custom-call(bf16[2,32,1664]{2,1,0:T(8,128)(2,1)} %q_ref.1, bf16[2,32,1664]{2,1,0:T(8,128)(2,1)} %k_ref.1, bf16[2,32,1664]{2,1,0:T(8,128)(2,1)} %v_ref.1, s32[1,128]{1,0:T(1,128)} %bitcast.17, s32[1,128]{1,0:T(1,128)} %bitcast.18, bf16[64,1664]{1,0:T(8,128)(2,1)} %hin_ref.1, ...), custom_call_target="tpu_custom_call" | custom-call | tf_op jit(solution)/shard_map/pallas_call | solution.py:292
  272.5 1.7 copy.18
  274.1 1.6 copy.21
Async XLA Ops:
  7.2 84.2 %all-gather.6.cloned.1.call-start = ((), (), s32[]{:S(2)}) async-start(), calls=%async_computation.1 | async-start | bytes 3514368 | tf_op jit(solution)/shard_map/all_gather | solution.py:288
  7.9 126.2 %all-gather.4.cloned.1.call-start = ((), (), s32[]{:S(2)}) async-start(), calls=%async_computation | async-start | bytes 6230016 | tf_op jit(solution)/shard_map/all_gather | solution.py:286
Sparse Core Ops, SparseCore 0:
  10.6 80.7 all-gather.5
  93.2 40.8 all-gather.3

commit v2 on v1

--- a/solution.py
+++ b/solution.py
@@ -21,10 +21,11 @@
     return lax.broadcasted_iota(i32, shape, dim)
 
 
-def kernel(q_ref, k_ref, v_ref, seg_ref, own_ref, hin_ref, wout_ref, wm_ref,
+def kernel(q_ref, k_ref, v_ref, seg_ref, own_ref, hin_ref, wo_ref, wm_ref,
            hout_ref, dout_ref,
-           kv, qb, oh, tr, kx, vx, qx, m_s, acc_s, ob, orecv, hb, hrecv, fb, frecv, outg, drecv,
-           s0, r_kv, r_q, r_oh, ss, rs, dss, drs, so, ro, sh, rh, sf, rf, sd, rd):
+           kv, qb, oh, tr, kx, vx, qx, m_s, acc_s, ob, orecv, hb, hrecv, fb, frecv, outg, drecv, res, wo, wm,
+           s0, r_kv, r_q, r_oh, ss, rs, dss, drs, so, ro, sh, rh, sf, rf, sd, rd,
+           swz, rwz, smz, rmz, swx, rwx, smx, rmx, swy, rwy, swp, rwp):
     w = lax.axis_index("wide")
     n = lax.axis_index("narrow")
     x, z = w // Z, w % Z
@@ -80,9 +81,53 @@
     g64, p64 = iota((64, 64), 0), iota((64, 64), 1)
     perm = (p64 == 4 * (g64 & 15) + (g64 >> 4)).astype(bf16)
     hp = jnp.dot(perm, hin_ref[...], preferred_element_type=f32).astype(bf16)
-    hb[...] = jnp.zeros_like(hb)
-    for i in range(NN):
-        hb[i, :, 0:208] = hp[:, 208 * i:208 * i + 208]
+    a208, b208 = iota((208, 256), 0), iota((208, 256), 1)
+    spread = ((a208 == 52 * (b208 >> 6) + (b208 & 63)) & ((b208 & 63) < 52)).astype(bf16)
+    for i in range(NN):
+        res[:, 256 * i:256 * i + 256] = jnp.dot(hp[:, 208 * i:208 * i + 208], spread,
+                                                preferred_element_type=f32).astype(bf16)
+
+    eye = (iota((64, 52), 0) == iota((64, 52), 1)).astype(bf16)
+    heads = (((b208 < HD) & (a208 == b208)) | ((b208 >= 128) & (b208 < 128 + HD) & (a208 == b208 - 24))).astype(bf16)
+    plain = (a208 == b208).astype(bf16)
+
+    def turned(block, lanes):
+        t = lax.dot_general(eye, block, (((1,), (1,)), ((), ())), preferred_element_type=f32).astype(bf16)
+        return jnp.dot(t, lanes, preferred_element_type=f32).astype(bf16)
+
+    wo[n, w] = turned(wo_ref[...], heads)
+    for j in range(4):
+        wm[w, j] = turned(wm_ref[j], plain)
+
+    def wo_rows(dx):
+        return pl.ds(pl.multiple_of(Z * ((x - dx + X) % X), Z), Z)
+
+    def wo_z(d):
+        return remote(wo.at[n, w], wo.at[n, w], swz.at[d], rwz.at[d], x * Z + (z + d) % Z, n)
+
+    def wm_z(d):
+        return remote(wm.at[w], wm.at[w], smz.at[d], rmz.at[d], x * Z + (z + d) % Z, n)
+
+    def wo_x(dx):
+        ref = wo.at[n, wo_rows(0)]
+        return remote(ref, ref, swx.at[dx], rwx.at[dx], ((x + dx) % X) * Z + z, n)
+
+    def wm_x(d, dx):
+        ref = wm.at[x * Z + (z - d + Z) % Z]
+        return remote(ref, ref, smx.at[4 * d + dx], rmx.at[4 * d + dx], ((x + dx) % X) * Z + z, n)
+
+    def wo_y(dx, dy):
+        ref = wo.at[n, wo_rows(dx)]
+        return remote(ref, ref, swy.at[4 * dx + dy], rwy.at[4 * dx + dy], w, 2 * ((y + dy) % Y) + c)
+
+    def wo_p(dx, dy):
+        ref = wo.at[2 * ((y - dy + Y) % Y) + c, wo_rows(dx)]
+        return remote(ref, ref, swp.at[4 * dx + dy], rwp.at[4 * dx + dy], w, n + up)
+
+    def wo_on(dx):
+        for dy in range(1, Y):
+            wo_y(dx, dy).start()
+        wo_p(dx, 0).start()
 
     owner_row = own_ref[...]
     owner_col = jnp.broadcast_to(owner_row.astype(f32), (128, 128)).T
@@ -111,6 +156,10 @@
     for args in starts:
         send(*args)
 
+    @pl.loop(1, Z)
+    def _(d):
+        wo_z(d).start()
+
     m_s[...] = jnp.full_like(m_s, -3e38)
     acc_s[...] = jnp.zeros_like(acc_s)
 
@@ -170,6 +219,10 @@
     onward(0, 2).start()
     to_partner(z).start()
 
+    @pl.loop(1, Z)
+    def _(d):
+        wm_z(d).start()
+
     for i in range(X):
         arrived(qb.at[pl.ds(16 * i, 16)], r_q.at[i])
     lane16 = iota((16, 128), 1)
@@ -182,6 +235,14 @@
                 qj = piece(lambda t: qb[16 * i:16 * i + 16, 128 * t:128 * t + 128], j)
                 qx[256 * i + 16 * j:256 * i + 16 * j + 16, :] = jnp.where(lane16 < HD, qj, ohr)
 
+    @pl.loop(1, Z)
+    def _(d):
+        arrived(wo.at[n, x * Z + (z - d + Z) % Z], rwz.at[d])
+    for dx in range(1, X):
+        wo_x(dx).start()
+        wm_x(0, dx).start()
+    wo_on(0)
+
     @pl.loop(0, Z)
     def _(k):
         def take(kk):
@@ -204,6 +265,25 @@
         arrived(kv.at[1 - c, slot], drs.at[slot])
         attend(slot)
 
+        @pl.when(k >= 1)
+        def _():
+            h = (k + 1) // 2
+            d = jnp.where(k % 2 == 1, h, Z - h)
+            arrived(wm.at[x * Z + (z - d + Z) % Z], rmz.at[d])
+            for dx in range(1, X):
+                wm_x(d, dx).start()
+
+        @pl.when((k >= 1) & (k < X))
+        def _():
+            arrived(wo.at[n, wo_rows(k)], rwx.at[k])
+            wo_on(k)
+
+        @pl.when(k >= X)
+        def _():
+            for dy in range(1, Y):
+                arrived(wo.at[2 * ((y - dy + Y) % Y) + c, wo_rows(k - X)], rwy.at[4 * (k - X) + dy])
+                wo_p(k - X, dy).start()
+
     i0, i1 = iota((256, 256), 0), iota((256, 256), 1)
     grp, pos = i0 & 15, (i0 >> 4) & 3
     r_src = 4 * (i0 >> 6) + (grp >> 2)
@@ -219,14 +299,22 @@
         for l in range(4):
             send(ob.at[4 * i + l], orecv.at[head], so.at[4 * i + l], ro.at[head], i * Z + z, 4 * c + l)
 
+    @pl.loop(0, X)
+    def _(dx):
+        for dy in range(Y):
+            arrived(wo.at[2 * ((y - dy + Y) % Y) + 1 - c, wo_rows(dx)], rwp.at[4 * dx + dy])
     hid = jnp.zeros((64, TILE), f32)
-    for hp2 in range(8):
-        arrived(orecv.at[2 * hp2], ro.at[2 * hp2])
-        arrived(orecv.at[2 * hp2 + 1], ro.at[2 * hp2 + 1])
-        a = jnp.concatenate([orecv[2 * hp2], orecv[2 * hp2 + 1]], axis=1)
-        hid = hid + jnp.dot(a, wout_ref[256 * hp2:256 * hp2 + 256, :], preferred_element_type=f32)
-    for i in range(NN):
-        hb[i] = (hb[i].astype(f32) + hid[:, 256 * i:256 * i + 256]).astype(bf16)
+    for i in range(NN):
+        arrived(orecv.at[2 * i], ro.at[2 * i])
+        arrived(orecv.at[2 * i + 1], ro.at[2 * i + 1])
+        a = jnp.concatenate([orecv[2 * i], orecv[2 * i + 1]], axis=1)
+        hid = hid + lax.dot_general(a, wo[i].reshape(TILE, 256), (((1,), (1,)), ((), ())),
+                                    preferred_element_type=f32)
+    a256, b256 = iota((256, 256), 0), iota((256, 256), 1)
+    narrowed = ((b256 == 52 * (a256 >> 6) + (a256 & 63)) & ((a256 & 63) < 52)).astype(bf16)
+    for i in range(NN):
+        h = (res[:, 256 * i:256 * i + 256].astype(f32) + hid[:, 256 * i:256 * i + 256]).astype(bf16)
+        hb[i] = jnp.dot(h, narrowed, preferred_element_type=f32).astype(bf16)
     for i in range(NN):
         send(hb.at[i], hrecv.at[n], sh.at[i], rh.at[n], w, i)
     whole = jnp.concatenate([hb[i][:, 0:208] for i in range(NN)], axis=1)
@@ -235,10 +323,15 @@
 
     for i in range(NN):
         arrived(hrecv.at[i], rh.at[i])
+    @pl.loop(0, Z)
+    def _(d):
+        for dx in range(1, X):
+            arrived(wm.at[Z * ((x - dx + X) % X) + (z - d + Z) % Z], rmx.at[4 * d + dx])
     part = jnp.zeros((128, TILE), f32)
     for j in range(4):
-        part = part + jnp.dot(hrecv[:, 16 * j:16 * j + 16, :].reshape(128, 256), wm_ref[j],
-                              preferred_element_type=f32)
+        part = part + lax.dot_general(hrecv[:, 16 * j:16 * j + 16, :].reshape(128, 256),
+                                      wm[:, j].reshape(TILE, 256), (((1,), (1,)), ((), ())),
+                                      preferred_element_type=f32)
     for i in range(NN):
         fb[i] = part[:, 256 * i:256 * i + 256].astype(bf16)
     for i in range(NN):
@@ -248,6 +341,7 @@
         arrived(frecv.at[i], rf.at[i])
         feat = feat + frecv[i].astype(f32)
 
+    feat = jnp.dot(feat.astype(bf16), narrowed, preferred_element_type=f32)
     outg[...] = jnp.dot(picker, feat.astype(bf16), preferred_element_type=f32).reshape(NW, 8, 256).astype(bf16)
 
     @pl.loop(0, NW)
@@ -265,6 +359,22 @@
     @pl.loop(1, Z)
     def _(t):
         onward(jnp.maximum(t - 2, 0), t).wait_send()
+        wo_z(t).wait_send()
+        wm_z(t).wait_send()
+    for dx in range(1, X):
+        wo_x(dx).wait_send()
+
+    @pl.loop(0, Z)
+    def _(d):
+        for dx in range(1, X):
+            wm_x(d, dx).wait_send()
+
+    @pl.loop(0, X)
+    def _(dx):
+        wo_p(dx, 0).wait_send()
+        for dy in range(1, Y):
+            wo_y(dx, dy).wait_send()
+            wo_p(dx, dy).wait_send()
 
     @pl.loop(0, Z)
     def _(t):
@@ -282,11 +392,6 @@
 
 
 def shards(hidden_in, queries, keys, values, out_weight, merge_weight, segment_ids, owners):
-    wout = lax.all_gather(out_weight, "wide", axis=1, tiled=True)
-    wout = lax.all_gather(wout, "narrow", axis=0, tiled=True)
-    wout = jnp.pad(wout.reshape(16, HD, NN, 208), ((0, 0), (0, 24), (0, 0), (0, 48))).reshape(TILE, TILE)
-    wm = lax.all_gather(merge_weight, "wide", axis=2, tiled=True)
-    wm = jnp.pad(wm.reshape(4, 208, NN, 208), ((0, 0), (0, 48), (0, 0), (0, 48))).reshape(4, 256, TILE)
     vm = pl.BlockSpec(memory_space=pltpu.VMEM)
     dma = pltpu.SemaphoreType.DMA
     return pl.pallas_call(
@@ -312,14 +417,19 @@
             pltpu.VMEM((NN, 128, 256), bf16),
             pltpu.VMEM((NW, 8, 256), bf16),
             pltpu.VMEM((NW, 8, 256), bf16),
+            pltpu.VMEM((64, TILE), bf16),
+            pltpu.VMEM((NN, NW, 64, 256), bf16),
+            pltpu.VMEM((NW, 4, 64, 256), bf16),
             dma((12,)), dma((X,)), dma((X,)), dma((X,)),
             dma((Z,)), dma((Z,)), dma((Z,)), dma((Z,)),
             dma((16,)), dma((16,)), dma((NN,)), dma((NN,)), dma((NN,)), dma((NN,)),
             dma((NW,)), dma((NW,)),
+            dma((Z,)), dma((Z,)), dma((Z,)), dma((Z,)), dma((X,)), dma((X,)), dma((4 * Z,)), dma((4 * Z,)),
+            dma((16,)), dma((16,)), dma((16,)), dma((16,)),
         ],
         compiler_params=pltpu.CompilerParams(collective_id=0, has_side_effects=True,
                                              vmem_limit_bytes=60 * 1024 * 1024),
-    )(queries, keys, values, segment_ids.reshape(1, 128), owners.reshape(1, 128), hidden_in, wout, wm)
+    )(queries, keys, values, segment_ids.reshape(1, 128), owners.reshape(1, 128), hidden_in, out_weight, merge_weight)
 
 
 def solution(mesh):

time: 283 us -> 144 us (0.51)
  waiting for transfers between devices: 65.8 us -> 0 us
  local copies, waits for them, and re-layouts: 52.6 us -> 5.6 us
  blocking collectives: 44.2 us -> 0 us
  Pallas kernels: 106 us -> 137 us
  between operations: 14.1 us -> 0.65 us
    all_gather x2 -> x0, waiting for transfers between devices: 65.1 us -> none  [the longest x1 37.7 us: shards(): wm = lax.all_gather(merge_weight, 'wide', axis=2, tiled=True)]
    all_gather x1 -> x0, blocking collectives: 44.2 us -> none  [shards(): wout = lax.all_gather(out_weight, 'wide', axis=1, tiled=True)]
    pallas_call x1, Pallas kernels: 106 us -> 137 us  [shards(): pl.pallas_call(kernel, out_shape=(jax.ShapeDtypeStruct((64, D), bf16), ja...]
    reshape x3 -> x0, local copies, waits for them, and re-layouts: 27.4 us -> none  [the longest x1 14.7 us: shards(): wout.reshape(16, HD, NN, 208)]
    pad x2 -> x0, local copies, waits for them, and re-layouts: 10.1 us -> none  [the longest x1 7.56 us: shards(): jnp.pad(wout.reshape(16, HD, NN, 208), ((0, 0), (0, 24), (0, 0), (0, 48)))]
    unnamed x4 -> x5, local copies, waits for them, and re-layouts: 13.4 us -> 3.91 us
  transfers between devices with their start and end apart: 2 -> 0, of which waited for: 2 -> 0; matrix products, arithmetic and copies ran while one was open for 6% -> 0% of each run, Pallas kernels for 0% -> 0%
where the time goes in v2:
time: 144 us
  Pallas kernels  137 us (95%)
  local copies, waits for them, and re-layouts  5.6 us (4%)
    pallas_call x1, Pallas kernels, shards(): pl.pallas_call(kernel, out_shape=(jax.ShapeDtypeStruct((64, D), bf16), ja...  137 us
    unnamed x5, local copies, waits for them, and re-layouts  3.91 us

profile of v2, /device:TPU:1, one launch (start us, length us, event | category | flops | bytes accessed | tf_op | source)
XLA Modules:
  0.0 143.7 jit_solution(607047028567704424)
XLA Ops:
  0.6 1.5 %copy.10.wo_ref = bf16[208,52]{1,0:T(8,128)(2,1)} copy(bf16[208,52]{0,1:T(8,128)(2,1)} %param.12) | data formatting | bytes 43264 | tf_op args[4]
  2.1 1.7 %copy.11.wm_ref = bf16[4,208,52]{2,1,0:T(8,128)(2,1)} copy(bf16[4,208,52]{1,0,2:T(4,128)(2,1)} %param.13) | data formatting | bytes 173056 | tf_op args[5]
  3.9 137.4 %shard_map.95 = (bf16[64,1664]{1,0:T(8,128)(2,1)}, bf16[256,208]{1,0:T(8,128)(2,1)}) custom-call(bf16[2,32,1664]{2,1,0:T(8,128)(2,1)} %q_ref.1, bf16[2,32,1664]{2,1,0:T(8,128)(2,1)} %k_ref.1, bf16[2,32,1664]{2,1,0:T(8,128)(2,1)} %v_ref.1, s32[1,128]{1,0:T(1,128)} %bitcast.2, s32[1,128]{1,0:T(1,128)} %bitcast.3, bf16[64,1664]{1,0:T(8,128)(2,1)} %hin_ref.1, ...), custom_call_target="tpu_custom_call" | custom-call | tf_op jit(solution)/shard_map/pallas_call | solution.py:397
  141.3 0.0 copy-start
  141.3 1.7 %copy.12 = bf16[256,208]{0,1:T(8,128)(2,1)} copy(bf16[256,208]{1,0:T(8,128)(2,1)} %get-tuple-element.3) | data formatting | bytes 212992 | tf_op jit(solution)/shard_map/pallas_call | solution.py:397
  143.0 0.0 copy-done
  143.0 0.7 copy.14
Async XLA Ops:
  141.3 1.7 %copy-start = (bf16[64,1664]{1,0:T(8,128)(2,1)S(1)}, bf16[64,1664]{1,0:T(8,128)(2,1)}, u32[]{:S(2)}) copy-start(bf16[64,1664]{1,0:T(8,128)(2,1)} %get-tuple-element.6) | copy-start | bytes 638980

commit v3 on v2

--- a/solution.py
+++ b/solution.py
@@ -105,29 +105,76 @@
     def wo_z(d):
         return remote(wo.at[n, w], wo.at[n, w], swz.at[d], rwz.at[d], x * Z + (z + d) % Z, n)
 
-    def wm_z(d):
-        return remote(wm.at[w], wm.at[w], smz.at[d], rmz.at[d], x * Z + (z + d) % Z, n)
+    def slot_at(k):
+        h = (k + 1) // 2
+        sign = jnp.where(k % 2 == 1, -1, 1)
+        return (z + sign * up * h + 2 * Z) % Z
+
+    def wm_z(k, t):
+        ref = wm.at[x * Z + slot_at(k)]
+        dz = (z + jnp.where(t % 2 == 1, up, -up) + Z) % Z
+        return remote(ref, ref, smz.at[t], rmz.at[t], x * Z + dz, n)
+
+    def half_rows(dx, i):
+        return pl.ds(pl.multiple_of(Z * ((x - dx + X) % X) + 4 * i, 4), 4)
 
     def wo_x(dx):
         ref = wo.at[n, wo_rows(0)]
         return remote(ref, ref, swx.at[dx], rwx.at[dx], ((x + dx) % X) * Z + z, n)
 
-    def wm_x(d, dx):
-        ref = wm.at[x * Z + (z - d + Z) % Z]
-        return remote(ref, ref, smx.at[4 * d + dx], rmx.at[4 * d + dx], ((x + dx) % X) * Z + z, n)
+    def wo_xr(i):
+        ref = wo.at[n, half_rows(1 + 2 * i, i)]
+        return remote(ref, ref, swx.at[2 * i], rwx.at[2 * i], ((x + 1 + 2 * i) % X) * Z + z, n)
+
+    def wm_at(k, dx):
+        return wm.at[Z * ((x - dx + X) % X) + slot_at(k)]
+
+    def wm_half(k, dx, i):
+        return wm.at[Z * ((x - dx + X) % X) + slot_at(k), pl.ds(2 * i, 2)]
+
+    def wm_x(k, dx):
+        ref = wm_at(k, 0)
+        return remote(ref, ref, smx.at[4 * k + dx], rmx.at[4 * k + dx], ((x + dx) % X) * Z + z, n)
+
+    def wm_xr(k, i):
+        ref = wm_half(k, 1 + 2 * i, i)
+        return remote(ref, ref, smx.at[4 * k + 2 * i], rmx.at[4 * k + 2 * i], ((x + 1 + 2 * i) % X) * Z + z, n)
+
+    def wm_relay(k):
+        for i in range(2):
+            arrived(wm_at(k, 1 + 2 * i), rmx.at[4 * k + 1 + 2 * i])
+            wm_xr(k, i).start()
+
+    def narrow_at(dy):
+        return 2 * ((y - dy + Y) % Y) + c
 
     def wo_y(dx, dy):
         ref = wo.at[n, wo_rows(dx)]
         return remote(ref, ref, swy.at[4 * dx + dy], rwy.at[4 * dx + dy], w, 2 * ((y + dy) % Y) + c)
 
+    def wo_yr(dx, i):
+        ref = wo.at[narrow_at(1 + 2 * i), half_rows(dx, i)]
+        return remote(ref, ref, swy.at[4 * dx + 2 * i], rwy.at[4 * dx + 2 * i], w, 2 * ((y + 1 + 2 * i) % Y) + c)
+
     def wo_p(dx, dy):
-        ref = wo.at[2 * ((y - dy + Y) % Y) + c, wo_rows(dx)]
+        ref = wo.at[narrow_at(dy), wo_rows(dx)]
         return remote(ref, ref, swp.at[4 * dx + dy], rwp.at[4 * dx + dy], w, n + up)
 
     def wo_on(dx):
-        for dy in range(1, Y):
-            wo_y(dx, dy).start()
+        wo_y(dx, 1).start()
+        wo_y(dx, 3).start()
         wo_p(dx, 0).start()
+
+    def wo_relay(dx):
+        for i in range(2):
+            arrived(wo.at[narrow_at(1 + 2 * i), wo_rows(dx)], rwy.at[4 * dx + 1 + 2 * i])
+            wo_yr(dx, i).start()
+            wo_p(dx, 1 + 2 * i).start()
+
+    def wo_last(dx):
+        for i in range(2):
+            arrived(wo.at[narrow_at(2), half_rows(dx, i)], rwy.at[4 * dx + 2 * i])
+        wo_p(dx, 2).start()
 
     owner_row = own_ref[...]
     owner_col = jnp.broadcast_to(owner_row.astype(f32), (128, 128)).T
@@ -201,11 +248,6 @@
         arrived(kv.at[c, z, pl.ds(32 * i, 32), main], r_kv.at[i])
         arrived(kv.at[c, z, pl.ds(32 * i, 32), tail], r_oh.at[i])
 
-    def slot_at(k):
-        h = (k + 1) // 2
-        sign = jnp.where(k % 2 == 1, -1, 1)
-        return (z + sign * up * h + 2 * Z) % Z
-
     def to_partner(slot):
         return remote(kv.at[c, slot], kv.at[c, slot], dss.at[slot], drs.at[slot], w, n + up)
 
@@ -219,9 +261,8 @@
     onward(0, 2).start()
     to_partner(z).start()
 
-    @pl.loop(1, Z)
-    def _(d):
-        wm_z(d).start()
+    wm_z(0, 1).start()
+    wm_z(0, 2).start()
 
     for i in range(X):
         arrived(qb.at[pl.ds(16 * i, 16)], r_q.at[i])
@@ -238,7 +279,7 @@
     @pl.loop(1, Z)
     def _(d):
         arrived(wo.at[n, x * Z + (z - d + Z) % Z], rwz.at[d])
-    for dx in range(1, X):
+    for dx in (1, 3):
         wo_x(dx).start()
         wm_x(0, dx).start()
     wo_on(0)
@@ -267,22 +308,43 @@
 
         @pl.when(k >= 1)
         def _():
-            h = (k + 1) // 2
-            d = jnp.where(k % 2 == 1, h, Z - h)
-            arrived(wm.at[x * Z + (z - d + Z) % Z], rmz.at[d])
-            for dx in range(1, X):
-                wm_x(d, dx).start()
+            arrived(wm_at(k, 0), rmz.at[k])
+
+            @pl.when(k + 2 < Z)
+            def _():
+                wm_z(k, k + 2).start()
+            for dx in (1, 3):
+                wm_x(k, dx).start()
+
+        @pl.when(k == 1)
+        def _():
+            for i in range(2):
+                arrived(wo.at[n, wo_rows(1 + 2 * i)], rwx.at[1 + 2 * i])
+                wo_xr(i).start()
+
+        @pl.when(k == 3)
+        def _():
+            for i in range(2):
+                arrived(wo.at[n, half_rows(2, i)], rwx.at[2 * i])
+
+        def nth(i):
+            return i + jnp.where(i == 2, 1, 0) - jnp.where(i == 3, 1, 0)
 
         @pl.when((k >= 1) & (k < X))
         def _():
-            arrived(wo.at[n, wo_rows(k)], rwx.at[k])
-            wo_on(k)
-
-        @pl.when(k >= X)
-        def _():
-            for dy in range(1, Y):
-                arrived(wo.at[2 * ((y - dy + Y) % Y) + c, wo_rows(k - X)], rwy.at[4 * (k - X) + dy])
-                wo_p(k - X, dy).start()
+            wo_on(nth(k))
+
+        @pl.when((k >= 1) & (k < X + 1))
+        def _():
+            wo_relay(nth(k - 1))
+
+        @pl.when((k >= 2) & (k < X + 2))
+        def _():
+            wo_last(nth(k - 2))
+
+        @pl.when(k >= 1)
+        def _():
+            wm_relay(k - 1)
 
     i0, i1 = iota((256, 256), 0), iota((256, 256), 1)
     grp, pos = i0 & 15, (i0 >> 4) & 3
@@ -299,6 +361,8 @@
         for l in range(4):
             send(ob.at[4 * i + l], orecv.at[head], so.at[4 * i + l], ro.at[head], i * Z + z, 4 * c + l)
 
+    wm_relay(Z - 1)
+
     @pl.loop(0, X)
     def _(dx):
         for dy in range(Y):
@@ -324,9 +388,9 @@
     for i in range(NN):
         arrived(hrecv.at[i], rh.at[i])
     @pl.loop(0, Z)
-    def _(d):
-        for dx in range(1, X):
-            arrived(wm.at[Z * ((x - dx + X) % X) + (z - d + Z) % Z], rmx.at[4 * d + dx])
+    def _(k):
+        for i in range(2):
+            arrived(wm_half(k, 2, i), rmx.at[4 * k + 2 * i])
     part = jnp.zeros((128, TILE), f32)
     for j in range(4):
         part = part + lax.dot_general(hrecv[:, 16 * j:16 * j + 16, :].reshape(128, 256),
@@ -360,20 +424,23 @@
     def _(t):
         onward(jnp.maximum(t - 2, 0), t).wait_send()
         wo_z(t).wait_send()
-        wm_z(t).wait_send()
-    for dx in range(1, X):
-        wo_x(dx).wait_send()
+        wm_z(jnp.maximum(t - 2, 0), t).wait_send()
+    for i in range(2):
+        wo_x(1 + 2 * i).wait_send()
+        wo_xr(i).wait_send()
 
     @pl.loop(0, Z)
-    def _(d):
-        for dx in range(1, X):
-            wm_x(d, dx).wait_send()
+    def _(k):
+        for i in range(2):
+            wm_x(k, 1 + 2 * i).wait_send()
+            wm_xr(k, i).wait_send()
 
     @pl.loop(0, X)
     def _(dx):
-        wo_p(dx, 0).wait_send()
-        for dy in range(1, Y):
-            wo_y(dx, dy).wait_send()
+        for i in range(2):
+            wo_y(dx, 1 + 2 * i).wait_send()
+            wo_yr(dx, i).wait_send()
+        for dy in range(Y):
             wo_p(dx, dy).wait_send()
 
     @pl.loop(0, Z)

time: 144 us -> 134 us (0.931)
  Pallas kernels: 137 us -> 128 us
    pallas_call x1, Pallas kernels: 137 us -> 128 us  [shards(): pl.pallas_call(kernel, out_shape=(jax.ShapeDtypeStruct((64, D), bf16), ja...]
where the time goes in v3:
time: 134 us
  Pallas kernels  128 us (96%)
  local copies, waits for them, and re-layouts  5.6 us (4%)
    pallas_call x1, Pallas kernels, shards(): pl.pallas_call(kernel, out_shape=(jax.ShapeDtypeStruct((64, D), bf16), ja...  128 us
    unnamed x5, local copies, waits for them, and re-layouts  3.91 us

profile of v3, /device:TPU:1, one launch (start us, length us, event | category | flops | bytes accessed | tf_op | source)
XLA Modules:
  0.0 134.2 jit_solution(90446654694061819)
XLA Ops:
  0.6 1.5 %copy.10.wo_ref = bf16[208,52]{1,0:T(8,128)(2,1)} copy(bf16[208,52]{0,1:T(8,128)(2,1)} %param.12) | data formatting | bytes 43264 | tf_op args[4]
  2.1 1.7 %copy.11.wm_ref = bf16[4,208,52]{2,1,0:T(8,128)(2,1)} copy(bf16[4,208,52]{1,0,2:T(4,128)(2,1)} %param.13) | data formatting | bytes 173056 | tf_op args[5]
  3.9 128.0 %shard_map.95 = (bf16[64,1664]{1,0:T(8,128)(2,1)}, bf16[256,208]{1,0:T(8,128)(2,1)}) custom-call(bf16[2,32,1664]{2,1,0:T(8,128)(2,1)} %q_ref.1, bf16[2,32,1664]{2,1,0:T(8,128)(2,1)} %k_ref.1, bf16[2,32,1664]{2,1,0:T(8,128)(2,1)} %v_ref.1, s32[1,128]{1,0:T(1,128)} %bitcast.2, s32[1,128]{1,0:T(1,128)} %bitcast.3, bf16[64,1664]{1,0:T(8,128)(2,1)} %hin_ref.1, ...), custom_call_target="tpu_custom_call" | custom-call | tf_op jit(solution)/shard_map/pallas_call | solution.py:464
  131.9 0.0 copy-start
  131.9 1.7 %copy.12 = bf16[256,208]{0,1:T(8,128)(2,1)} copy(bf16[256,208]{1,0:T(8,128)(2,1)} %get-tuple-element.3) | data formatting | bytes 212992 | tf_op jit(solution)/shard_map/pallas_call | solution.py:464
  133.6 0.0 copy-done
  133.6 0.7 copy.14
Async XLA Ops:
  131.9 1.7 %copy-start = (bf16[64,1664]{1,0:T(8,128)(2,1)S(1)}, bf16[64,1664]{1,0:T(8,128)(2,1)}, u32[]{:S(2)}) copy-start(bf16[64,1664]{1,0:T(8,128)(2,1)} %get-tuple-element.6) | copy-start | bytes 638980

commit v4 on v3

--- a/solution.py
+++ b/solution.py
@@ -233,16 +233,21 @@
                 vj = piece(lambda t: kv[1, slot, :, 128 * t:128 * t + 128], j)
                 vx[128 * j:128 * j + 128, :] = jnp.where(lane < HD, vj, ones_col)
 
-        @pl.loop(0, X)
-        def _(qt):
-            rows = pl.ds(pl.multiple_of(256 * qt, 256), 256)
-            s = lax.dot_general(qx[rows, :], kx[...], (((1,), (1,)), ((), ())), preferred_element_type=f32)
+        def scores(qt):
+            return lax.dot_general(qx[256 * qt:256 * qt + 256, :], kx[...], (((1,), (1,)), ((), ())),
+                                   preferred_element_type=f32)
+
+        s = scores(0)
+        for qt in range(X):
+            s_next = scores(qt + 1) if qt + 1 < X else None
+            rows = slice(256 * qt, 256 * qt + 256)
             m_old = m_s[rows, :]
             m_new = jnp.maximum(m_old, jnp.max(s, axis=1, keepdims=True))
             p = jnp.exp2((s - m_new) * scale).astype(bf16)
             fix = jnp.exp2((m_old - m_new) * scale)
             acc_s[rows, :] = acc_s[rows, :] * fix + jnp.dot(p, vx[...], preferred_element_type=f32)
             m_s[rows, :] = m_new
+            s = s_next
 
     for i in range(X):
         arrived(kv.at[c, z, pl.ds(32 * i, 32), main], r_kv.at[i])

time: 134 us -> 127 us (0.948)
  Pallas kernels: 128 us -> 120 us
    pallas_call x1, Pallas kernels: 128 us -> 120 us  [shards(): pl.pallas_call(kernel, out_shape=(jax.ShapeDtypeStruct((64, D), bf16), ja...]
where the time goes in v4:
time: 127 us
  Pallas kernels  120 us (94%)
  local copies, waits for them, and re-layouts  5.6 us (4%)
    pallas_call x1, Pallas kernels, shards(): pl.pallas_call(kernel, out_shape=(jax.ShapeDtypeStruct((64, D), bf16), ja...  120 us
    unnamed x5, local copies, waits for them, and re-layouts  3.91 us

profile of v4, /device:TPU:1, one launch (start us, length us, event | category | flops | bytes accessed | tf_op | source)
XLA Modules:
  0.0 126.7 jit_solution(7288009041028103982)
XLA Ops:
  0.6 1.5 %copy.10.wo_ref = bf16[208,52]{1,0:T(8,128)(2,1)} copy(bf16[208,52]{0,1:T(8,128)(2,1)} %param.12) | data formatting | bytes 43264 | tf_op args[4]
  2.1 1.7 %copy.11.wm_ref = bf16[4,208,52]{2,1,0:T(8,128)(2,1)} copy(bf16[4,208,52]{1,0,2:T(4,128)(2,1)} %param.13) | data formatting | bytes 173056 | tf_op args[5]
  3.9 120.5 %shard_map.95 = (bf16[64,1664]{1,0:T(8,128)(2,1)}, bf16[256,208]{1,0:T(8,128)(2,1)}) custom-call(bf16[2,32,1664]{2,1,0:T(8,128)(2,1)} %q_ref.1, bf16[2,32,1664]{2,1,0:T(8,128)(2,1)} %k_ref.1, bf16[2,32,1664]{2,1,0:T(8,128)(2,1)} %v_ref.1, s32[1,128]{1,0:T(1,128)} %bitcast.2, s32[1,128]{1,0:T(1,128)} %bitcast.3, bf16[64,1664]{1,0:T(8,128)(2,1)} %hin_ref.1, ...), custom_call_target="tpu_custom_call" | custom-call | tf_op jit(solution)/shard_map/pallas_call | solution.py:469
  124.4 0.0 copy-start
  124.4 1.7 %copy.12 = bf16[256,208]{0,1:T(8,128)(2,1)} copy(bf16[256,208]{1,0:T(8,128)(2,1)} %get-tuple-element.3) | data formatting | bytes 212992 | tf_op jit(solution)/shard_map/pallas_call | solution.py:469
  126.1 0.0 copy-done
  126.1 0.7 copy.14
Async XLA Ops:
  124.4 1.7 %copy-start = (bf16[64,1664]{1,0:T(8,128)(2,1)S(1)}, bf16[64,1664]{1,0:T(8,128)(2,1)}, u32[]{:S(2)}) copy-start(bf16[64,1664]{1,0:T(8,128)(2,1)} %get-tuple-element.6) | copy-start | bytes 638980
